TPU v7x, 32 devices: a whole 2x2x4 slice. The times are simulated.
32 devices in a mesh: pole: 4 (over y, x), row: 8 (over z, core).
Axes of the slice: x: 2, y: 2, z: 4, core: 2. Of those that a mesh axis runs over, the one named last changes fastest.
Arguments:
- basis: bfloat16 [32768, 128], P('row'), may hold values from -24 to 24
- inverses: bfloat16 [4, 64, 512, 512], P('pole', 'row'), may hold values from -1.5 to 1.5
- lower: bfloat16 [64, 512, 512], P('row'), may hold values from -0.03955078 to 0.03955078
- upper: bfloat16 [64, 512, 512], P('row'), may hold values from -0.03955078 to 0.03955078
- pole_weights: float32 [4], P('pole'), may hold values from 0.5 to 1.5
Outputs:
- new_basis: float32 [32768, 128], P(('row', 'pole'))
All inputs are finite; a program needn't handle non-finite values.
Results may differ from a plain program's by a relative error of at most 0.003.
Values may be sent and summed in bfloat16 or wider, within the bound.
A program may use at most 64 MiB of HBM per device.

v0:
```python
import jax
import jax.numpy as jnp
from jax import lax
from jax.sharding import PartitionSpec as P

SWEEPS = 4


def padded_2(value, sides, width):
    for axis, dim in sides:
        peers, length = (lax.axis_size(axis), value.shape[dim])
        up = [(i, (i + 1) % peers) for i in range(peers - 1)]
        down = [(j, i) for i, j in up]
        last = lax.slice_in_dim(value, length - width, length, axis=dim)
        initial = lax.slice_in_dim(value, 0, width, axis=dim)
        before = lax.ppermute(last, axis, up)
        after = lax.ppermute(initial, axis, down)
        value = jnp.concatenate([before, value, after], axis=dim)
    return value


def shards(basis, inverses, lower, upper, pole_weights):
    rows, width = basis.shape
    count = inverses.shape[1]
    size = inverses.shape[-1]
    inverse = inverses[0]
    blocks = basis.reshape(count, size, width)
    state = jnp.einsum("bij,bjk->bik", inverse, blocks, preferred_element_type=jnp.float32).astype(
        jnp.bfloat16
    )
    for sweep in range(SWEEPS):
        padded = padded_2(state.reshape(rows, width), (("row", 0),), size)
        padded = padded.reshape(count + 2, size, width)
        rhs = blocks.astype(jnp.float32)
        rhs = rhs + jnp.einsum(
            "bij,bjk->bik", lower, padded[:-2], preferred_element_type=jnp.float32
        )
        rhs = rhs + jnp.einsum(
            "bij,bjk->bik", upper, padded[2:], preferred_element_type=jnp.float32
        )
        state = jnp.einsum(
            "bij,bjk->bik", inverse, rhs.astype(jnp.bfloat16), preferred_element_type=jnp.float32
        ).astype(jnp.bfloat16)
    weighted = pole_weights[0] * state.reshape(rows, width).astype(jnp.float32)
    total_rows = rows * lax.axis_size("row")
    filtered = lax.psum(weighted, "pole")
    share = rows // lax.axis_size("pole")
    mine = lax.dynamic_slice_in_dim(filtered, lax.axis_index("pole") * share, share, 0)
    partial_gram = jnp.dot(filtered.T, filtered, precision=lax.Precision.HIGHEST)
    gram = lax.psum(partial_gram, "row")
    gram = gram / total_rows
    factor = jnp.linalg.cholesky(gram)
    solved = jax.scipy.linalg.solve_triangular(factor, mine.T, lower=True)
    return solved.T


def solution(mesh):
    return jax.shard_map(
        shards,
        mesh=mesh,
        in_specs=(
            P("row", None),
            P("pole", "row", None, None),
            P("row", None, None),
            P("row", None, None),
            P("pole"),
        ),
        out_specs=P(("row", "pole"), None),
        check_vma=False,
    )
```

profile of v0, /device:TPU:0, one launch (start us, length us, event | category | flops | bytes accessed | tf_op | source)
XLA Modules:
  0.0 268.5 jit_solution(1977090597358284194)
XLA Ops:
  6.5 3.8 %fusion.18 = bf16[8,512,128]{2,1,0:T(8,128)(2,1)S(1)} fusion(bf16[8,512,128]{2,1,0:T(8,128)(2,1)} %bitcast.142, bf16[1,8,512,512]{3,2,1,0:T(8,128)(2,1)} %param.6), kind=kOutput, calls=%fused_computation.23 | convolution fusion | flops 537395200 | bytes 6291456 | tf_op jit(solution)/shard_map/bij,bjk->bik/dot_general | solution.py:28
  10.4 2.4 collective-permute-start
  14.7 3.7 %collective-permute-done.1 = bf16[512,128]{1,0:T(8,128)(2,1)} collective-permute-done((bf16[512,128]{1,0:T(8,128)(2,1)S(1)}, bf16[512,128]{1,0:T(8,128)(2,1)}, u32[]{:S(2)}, u32[]{:S(2)}) %collective-permute-start.1) | collective-permute-done | bytes 131104 | tf_op jit(solution)/shard_map/ppermute | solution.py:17
  18.4 2.0 pad_maximum_fusion.6
  20.4 3.7 %fusion.50 = f32[8,128,512]{2,1,0:T(8,128)S(1)} fusion(bf16[8,512,128]{2,1,0:T(8,128)(2,1)S(1)} %bitcast.131, bf16[8,512,512]{2,1,0:T(8,128)(2,1)} %param.7), kind=kOutput, calls=%fused_computation.60 | convolution fusion | flops 536870912 | bytes 7340032 | tf_op jit(solution)/shard_map/bij,bjk->bik/dot_general | solution.py:35
  24.1 7.6 %fusion.41 = bf16[8,512,128]{1,2,0:T(8,128)(2,1)} fusion(bf16[1,8,512,512]{3,2,1,0:T(8,128)(2,1)} %param.6, bf16[8,512,128]{1,2,0:T(8,128)(2,1)S(1)} %copy.15, f32[8,128,512]{2,1,0:T(8,128)S(1)} %fusion.50, bf16[8,512,128]{2,1,0:T(8,128)(2,1)} %bitcast.138, bf16[8,512,512]{2,1,0:T(8,128)(2,1)} %param.8), kind=kOutput, calls=%fused_computation.30 | convolution fusion | flops 1076363264 | bytes 13631488 | tf_op jit(solution)/shard_map/bij,bjk->bik/dot_general | solution.py:41
  32.7 5.4 %collective-permute-start.2 = (bf16[512,128]{0,1:T(8,128)(2,1)S(1)}, bf16[512,128]{0,1:T(8,128)(2,1)S(1)}, u32[]{:S(2)}, u32[]{:S(2)}) collective-permute-start(bf16[512,128]{0,1:T(8,128)(2,1)S(1)} %get-tuple-element.16), channel_id=1, source_target_pairs={{0,1},{1,2},{2,3},{3,4},{4,5},{5,6},{6,7},{8,9},{9,10},{10,11},{11... | collective-permute-start | bytes 393224 | tf_op jit(solution)/shard_map/ppermute | solution.py:16
  39.4 1.6 copy.16
  42.6 3.7 %fusion.51 = f32[8,128,512]{2,1,0:T(8,128)S(1)} fusion(bf16[8,512,128]{2,1,0:T(8,128)(2,1)S(1)} %bitcast.132, bf16[8,512,512]{2,1,0:T(8,128)(2,1)} %param.7), kind=kOutput, calls=%fused_computation.61 | convolution fusion | flops 536870912 | bytes 7340032 | tf_op jit(solution)/shard_map/bij,bjk->bik/dot_general | solution.py:35
  46.3 7.6 %fusion.38 = bf16[8,512,128]{1,2,0:T(8,128)(2,1)} fusion(bf16[1,8,512,512]{3,2,1,0:T(8,128)(2,1)} %param.6, bf16[8,512,128]{1,2,0:T(8,128)(2,1)S(1)} %copy.15, f32[8,128,512]{2,1,0:T(8,128)S(1)} %fusion.51, bf16[8,512,128]{2,1,0:T(8,128)(2,1)} %bitcast.139, bf16[8,512,512]{2,1,0:T(8,128)(2,1)} %param.8), kind=kOutput, calls=%fused_computation.29 | convolution fusion | flops 1076363264 | bytes 13631488 | tf_op jit(solution)/shard_map/bij,bjk->bik/dot_general | solution.py:41
  55.0 5.0 %collective-permute-start.4 = (bf16[512,128]{0,1:T(8,128)(2,1)S(1)}, bf16[512,128]{0,1:T(8,128)(2,1)S(1)}, u32[]{:S(2)}, u32[]{:S(2)}) collective-permute-start(bf16[512,128]{0,1:T(8,128)(2,1)S(1)} %get-tuple-element.12), channel_id=1, source_target_pairs={{0,1},{1,2},{2,3},{3,4},{4,5},{5,6},{6,7},{8,9},{9,10},{10,11},{11... | collective-permute-start | bytes 393224 | tf_op jit(solution)/shard_map/ppermute | solution.py:16
  61.2 1.6 copy.19
  64.4 3.7 %fusion.52 = f32[8,128,512]{2,1,0:T(8,128)S(1)} fusion(bf16[8,512,128]{2,1,0:T(8,128)(2,1)S(1)} %bitcast.133, bf16[8,512,512]{2,1,0:T(8,128)(2,1)} %param.7), kind=kOutput, calls=%fused_computation.62 | convolution fusion | flops 536870912 | bytes 7340032 | tf_op jit(solution)/shard_map/bij,bjk->bik/dot_general | solution.py:35
  68.1 7.6 %fusion.35 = bf16[8,512,128]{1,2,0:T(8,128)(2,1)} fusion(bf16[1,8,512,512]{3,2,1,0:T(8,128)(2,1)} %param.6, bf16[8,512,128]{1,2,0:T(8,128)(2,1)S(1)} %copy.15, f32[8,128,512]{2,1,0:T(8,128)S(1)} %fusion.52, bf16[8,512,128]{2,1,0:T(8,128)(2,1)} %bitcast.140, bf16[8,512,512]{2,1,0:T(8,128)(2,1)} %param.8), kind=kOutput, calls=%fused_computation.28 | convolution fusion | flops 1076363264 | bytes 13631488 | tf_op jit(solution)/shard_map/bij,bjk->bik/dot_general | solution.py:41
  76.7 5.0 %collective-permute-start.6 = (bf16[512,128]{0,1:T(8,128)(2,1)S(1)}, bf16[512,128]{0,1:T(8,128)(2,1)S(1)}, u32[]{:S(2)}, u32[]{:S(2)}) collective-permute-start(bf16[512,128]{0,1:T(8,128)(2,1)S(1)} %get-tuple-element.8), channel_id=1, source_target_pairs={{0,1},{1,2},{2,3},{3,4},{4,5},{5,6},{6,7},{8,9},{9,10},{10,11},{11... | collective-permute-start | bytes 393224 | tf_op jit(solution)/shard_map/ppermute | solution.py:16
  86.9 3.7 %fusion.53 = f32[8,128,512]{2,1,0:T(8,128)S(1)} fusion(bf16[8,512,128]{2,1,0:T(8,128)(2,1)S(1)} %bitcast.134, bf16[8,512,512]{2,1,0:T(8,128)(2,1)} %param.7), kind=kOutput, calls=%fused_computation.63 | convolution fusion | flops 536870912 | bytes 7340032 | tf_op jit(solution)/shard_map/bij,bjk->bik/dot_general | solution.py:35
  90.6 8.0 %multiply_bitcast_fusion = f32[8,512,128]{1,2,0:T(8,128)} fusion(bf16[1,8,512,512]{3,2,1,0:T(8,128)(2,1)} %param.6, bf16[8,512,128]{1,2,0:T(8,128)(2,1)S(1)} %copy.15, f32[8,128,512]{2,1,0:T(8,128)S(1)} %fusion.53, bf16[8,512,128]{2,1,0:T(8,128)(2,1)} %bitcast.130, bf16[8,512,512]{2,1,0:T(8,128)(2,1)} %param.8, f32[]{:T(128)} %bitcast.128), kind=kOutput, calls=%fused_computation.22 | convolution fusion | flops 1077411840 | bytes 14680068 | tf_op jit(solution)/shard_map/bij,bjk->bik/dot_general | solution.py:41
  98.5 2.9 %copy.25 = f32[8,512,128]{2,1,0:T(8,128)} copy(f32[8,512,128]{1,2,0:T(8,128)} %multiply_bitcast_fusion) | data formatting | bytes 4194304 | tf_op jit(solution)/shard_map/mul | solution.py:44
  101.5 71.8 %all-reduce.3.cloned.1.call-done = f32[4096,128]{1,0:T(8,128)} async-done(((f32[4096,128]{1,0:T(8,128)}), f32[4096,128]{1,0:T(8,128)}) %all-reduce.3.cloned.1.call-update) | async-done | bytes 2097168 | tf_op jit(solution)/shard_map/psum | solution.py:46
  173.4 6.3 %fusion.54 = f32[128,128]{0,1:T(8,128)} fusion(f32[4096,128]{1,0:T(8,128)} %all-reduce.3.cloned.1.call-done), kind=kOutput, calls=%fused_computation.64 | convolution fusion | flops 805306368 | bytes 2162688 | tf_op jit(solution)/shard_map/dot_general | solution.py:49
  179.7 54.8 %all-reduce.5.cloned.1.call-done = f32[128,128]{0,1:T(8,128)} async-done(((f32[128,128]{0,1:T(8,128)}), f32[128,128]{0,1:T(8,128)}) %all-reduce.5.cloned.1.call-update) | async-done | bytes 65552 | tf_op jit(solution)/shard_map/psum | solution.py:50
  236.3 11.7 %cholesky.16 = f32[128,128]{1,0:T(8,128)S(1)} custom-call(f32[128,128]{1,0:T(8,128)S(1)} %fusion.48), custom_call_target="Cholesky" | custom-call | tf_op jit(solution)/shard_map/jit(cholesky)/cholesky | solution.py:52
  249.4 9.8 %custom-call.7 = f32[1,128,128]{1,2,0:T(8,128)S(1)} custom-call(f32[1,128,128]{2,1,0:T(8,128)S(1)} %fusion.46), custom_call_target="InvertDiagBlocksLowerTriangular" | custom-call | tf_op jit(solution)/shard_map/jit(_solve_triangular)/triangular_solve | solution.py:53
  259.2 2.4 fusion.44
  (38 shorter events, 18.1 us)
Async XLA Ops:
  6.5 166.8 %all-reduce.3.cloned.1.call-start = ((), (), s32[]{:S(2)}) async-start(), calls=%async_computation | async-start | bytes 4194304 | tf_op jit(solution)/shard_map/psum | solution.py:46
  6.5 7.6 %copy-start = (bf16[4096,128]{1,0:T(8,128)(2,1)S(1)}, bf16[4096,128]{1,0:T(8,128)(2,1)}, u32[]{:S(2)}) copy-start(bf16[4096,128]{1,0:T(8,128)(2,1)} %param.5) | copy-start | bytes 3145732
  10.4 4.3 %collective-permute-start = (bf16[512,128]{1,0:T(8,128)(2,1)S(1)}, bf16[512,128]{1,0:T(8,128)(2,1)S(1)}, u32[]{:S(2)}, u32[]{:S(2)}) collective-permute-start(bf16[512,128]{1,0:T(8,128)(2,1)S(1)} %get-tuple-element.20), channel_id=1, source_target_pairs={{0,1},{1,2},{2,3},{3,4},{4,5},{5,6},{6,7},{8,9},{9,10},{10,11},{11... | collective-permute-start | bytes 393224 | tf_op jit(solution)/shard_map/ppermute | solution.py:16
  12.8 5.5 %collective-permute-start.1 = (bf16[512,128]{1,0:T(8,128)(2,1)S(1)}, bf16[512,128]{1,0:T(8,128)(2,1)}, u32[]{:S(2)}, u32[]{:S(2)}) collective-permute-start(bf16[512,128]{1,0:T(8,128)(2,1)S(1)} %get-tuple-element.19), channel_id=1, source_target_pairs={{1,0},{2,1},{3,2},{4,3},{5,4},{6,5},{7,6},{9,8},{10,9},{11,10},{12... | collective-permute-start | bytes 393224 | tf_op jit(solution)/shard_map/ppermute | solution.py:17
  32.7 8.4 %collective-permute-start.2 = (bf16[512,128]{0,1:T(8,128)(2,1)S(1)}, bf16[512,128]{0,1:T(8,128)(2,1)S(1)}, u32[]{:S(2)}, u32[]{:S(2)}) collective-permute-start(bf16[512,128]{0,1:T(8,128)(2,1)S(1)} %get-tuple-element.16), channel_id=1, source_target_pairs={{0,1},{1,2},{2,3},{3,4},{4,5},{5,6},{6,7},{8,9},{9,10},{10,11},{11... | collective-permute-start | bytes 393224 | tf_op jit(solution)/shard_map/ppermute | solution.py:16
  38.1 3.2 %collective-permute-start.3 = (bf16[512,128]{0,1:T(8,128)(2,1)S(1)}, bf16[512,128]{0,1:T(8,128)(2,1)S(1)}, u32[]{:S(2)}, u32[]{:S(2)}) collective-permute-start(bf16[512,128]{0,1:T(8,128)(2,1)S(1)} %get-tuple-element.15), channel_id=1, source_target_pairs={{1,0},{2,1},{3,2},{4,3},{5,4},{6,5},{7,6},{9,8},{10,9},{11,10},{12... | collective-permute-start | bytes 393224 | tf_op jit(solution)/shard_map/ppermute | solution.py:17
  55.0 7.9 %collective-permute-start.4 = (bf16[512,128]{0,1:T(8,128)(2,1)S(1)}, bf16[512,128]{0,1:T(8,128)(2,1)S(1)}, u32[]{:S(2)}, u32[]{:S(2)}) collective-permute-start(bf16[512,128]{0,1:T(8,128)(2,1)S(1)} %get-tuple-element.12), channel_id=1, source_target_pairs={{0,1},{1,2},{2,3},{3,4},{4,5},{5,6},{6,7},{8,9},{9,10},{10,11},{11... | collective-permute-start | bytes 393224 | tf_op jit(solution)/shard_map/ppermute | solution.py:16
  59.9 3.2 %collective-permute-start.5 = (bf16[512,128]{0,1:T(8,128)(2,1)S(1)}, bf16[512,128]{0,1:T(8,128)(2,1)S(1)}, u32[]{:S(2)}, u32[]{:S(2)}) collective-permute-start(bf16[512,128]{0,1:T(8,128)(2,1)S(1)} %get-tuple-element.11), channel_id=1, source_target_pairs={{1,0},{2,1},{3,2},{4,3},{5,4},{6,5},{7,6},{9,8},{10,9},{11,10},{12... | collective-permute-start | bytes 393224 | tf_op jit(solution)/shard_map/ppermute | solution.py:17
  76.7 8.7 %collective-permute-start.6 = (bf16[512,128]{0,1:T(8,128)(2,1)S(1)}, bf16[512,128]{0,1:T(8,128)(2,1)S(1)}, u32[]{:S(2)}, u32[]{:S(2)}) collective-permute-start(bf16[512,128]{0,1:T(8,128)(2,1)S(1)} %get-tuple-element.8), channel_id=1, source_target_pairs={{0,1},{1,2},{2,3},{3,4},{4,5},{5,6},{6,7},{8,9},{9,10},{10,11},{11... | collective-permute-start | bytes 393224 | tf_op jit(solution)/shard_map/ppermute | solution.py:16
  81.7 3.9 %collective-permute-start.7 = (bf16[512,128]{0,1:T(8,128)(2,1)S(1)}, bf16[512,128]{0,1:T(8,128)(2,1)S(1)}, u32[]{:S(2)}, u32[]{:S(2)}) collective-permute-start(bf16[512,128]{0,1:T(8,128)(2,1)S(1)} %get-tuple-element.7), channel_id=1, source_target_pairs={{1,0},{2,1},{3,2},{4,3},{5,4},{6,5},{7,6},{9,8},{10,9},{11,10},{12... | collective-permute-start | bytes 393224 | tf_op jit(solution)/shard_map/ppermute | solution.py:17
  101.5 133.1 %all-reduce.5.cloned.1.call-start = ((), (), s32[]{:S(2)}) async-start(), calls=%async_computation.1 | async-start | bytes 131072 | tf_op jit(solution)/shard_map/psum | solution.py:50
Sparse Core Ops, SparseCore 0:
  101.6 71.7 all-reduce.2
  179.8 54.6 all-reduce.4
where the time goes:
time: 269 us; the launch traced here: 268 us
  waiting for transfers between devices  131 us (49%)
  matrix products  58.2 us (22%)
  other arithmetic  29.9 us (11%)
  starting transfers between devices  23.2 us (9%)
  between operations  14.3 us (5%)
  local copies, waits for them, and re-layouts  12.1 us (4%)
    psum x1, waiting for transfers between devices, shards(): filtered = lax.psum(weighted, 'pole')  71.8 us
    psum x1, waiting for transfers between devices, shards(): gram = lax.psum(partial_gram, 'row')  54.8 us
    dot_general x4, matrix products, shards(): jnp.einsum('bij,bjk->bik', inverse, rhs.astype(jnp.bfloat16), preferred_e...  30.9 us
    ppermute x4, starting transfers between devices, padded_2(): before = lax.ppermute(last, axis, up)  17.8 us
    dot_general x4, matrix products, shards(): jnp.einsum('bij,bjk->bik', lower, padded[:-2], preferred_element_type=jnp...  14.8 us
    another operation x3, other arithmetic, shards(): factor = jnp.linalg.cholesky(gram)  12.4 us
    another operation x2, other arithmetic, shards(): solved = jax.scipy.linalg.solve_triangular(factor, mine.T, lower=True)  10.5 us
    dot_general x1, matrix products, shards(): jnp.dot(filtered.T, filtered, precision=lax.Precision.HIGHEST)  6.31 us
  transfers between devices with their start and end apart: 10, of which 5 were waited for; matrix products, arithmetic and copies ran while one was open for 2% of the time, Pallas kernels for 0%

commit v1 on v0

--- a/solution.py
+++ b/solution.py
@@ -4,6 +4,15 @@
 from jax.sharding import PartitionSpec as P
 
 SWEEPS = 4
+
+
+def doubling_sum(x, axis):
+    count = lax.axis_size(axis)
+    total, far = (x, 1)
+    while far < count:
+        total = total + lax.ppermute(total, axis, [(i, i ^ far) for i in range(count)])
+        far = 2 * far
+    return total
 
 
 def padded_2(value, sides, width):
@@ -43,7 +52,7 @@
         ).astype(jnp.bfloat16)
     weighted = pole_weights[0] * state.reshape(rows, width).astype(jnp.float32)
     total_rows = rows * lax.axis_size("row")
-    filtered = lax.psum(weighted, "pole")
+    filtered = doubling_sum(weighted, "pole")
     share = rows // lax.axis_size("pole")
     mine = lax.dynamic_slice_in_dim(filtered, lax.axis_index("pole") * share, share, 0)
     partial_gram = jnp.dot(filtered.T, filtered, precision=lax.Precision.HIGHEST)

time: 269 us -> 290 us (1.078)
  waiting for transfers between devices: 131 us -> 153 us
  matrix products: 58.2 us -> 55 us
  starting transfers between devices: 23.2 us -> 26.3 us
    ppermute x0 -> x2, waiting for transfers between devices: none -> 92.3 us  [doubling_sum(): lax.ppermute(total, axis, [(i, i ^ far) for i in range(count)])]
    psum x1 -> x0, waiting for transfers between devices: 71.8 us -> none  [shards(): filtered = lax.psum(weighted, 'pole')]
    ppermute x0 -> x2, starting transfers between devices: none -> 3.14 us  [doubling_sum(): lax.ppermute(total, axis, [(i, i ^ far) for i in range(count)])]
  transfers between devices with their start and end apart: 10 -> 11, of which waited for: 5 -> 6; matrix products, arithmetic and copies ran while one was open for 2% -> 2% of each run, Pallas kernels for 0% -> 0%
where the time goes in v1:
time: 290 us
  waiting for transfers between devices  153 us (53%)
  matrix products  55 us (19%)
  other arithmetic  30.4 us (10%)
  starting transfers between devices  26.3 us (9%)
  between operations  14.3 us (5%)
  local copies, waits for them, and re-layouts  11.1 us (4%)
    ppermute x2, waiting for transfers between devices, doubling_sum(): lax.ppermute(total, axis, [(i, i ^ far) for i in range(count)])  92.3 us
    psum x1, waiting for transfers between devices, shards(): gram = lax.psum(partial_gram, 'row')  56.3 us
    dot_general x4, matrix products, shards(): jnp.einsum('bij,bjk->bik', inverse, rhs.astype(jnp.bfloat16), preferred_e...  30.9 us
    ppermute x4, starting transfers between devices, padded_2(): before = lax.ppermute(last, axis, up)  17.8 us
    dot_general x4, matrix products, shards(): jnp.einsum('bij,bjk->bik', lower, padded[:-2], preferred_element_type=jnp...  14.8 us
    another operation x3, other arithmetic, shards(): factor = jnp.linalg.cholesky(gram)  12.4 us
    another operation x2, other arithmetic, shards(): solved = jax.scipy.linalg.solve_triangular(factor, mine.T, lower=True)  10.5 us
  transfers between devices with their start and end apart: 11, of which 6 were waited for; matrix products, arithmetic and copies ran while one was open for 2% of the time, Pallas kernels for 0%

profile of v1, /device:TPU:0, one launch (start us, length us, event | category | flops | bytes accessed | tf_op | source)
XLA Modules:
  0.0 289.6 jit_solution(17731752168820075530)
XLA Ops:
  6.5 3.8 %fusion.18 = bf16[8,512,128]{2,1,0:T(8,128)(2,1)S(1)} fusion(bf16[8,512,128]{2,1,0:T(8,128)(2,1)} %bitcast.143, bf16[1,8,512,512]{3,2,1,0:T(8,128)(2,1)} %param.6), kind=kOutput, calls=%fused_computation.23 | convolution fusion | flops 537395200 | bytes 6291456 | tf_op jit(solution)/shard_map/bij,bjk->bik/dot_general | solution.py:37
  10.4 2.4 collective-permute-start
  14.7 3.7 %collective-permute-done.1 = bf16[512,128]{1,0:T(8,128)(2,1)} collective-permute-done((bf16[512,128]{1,0:T(8,128)(2,1)S(1)}, bf16[512,128]{1,0:T(8,128)(2,1)}, u32[]{:S(2)}, u32[]{:S(2)}) %collective-permute-start.1) | collective-permute-done | bytes 131104 | tf_op jit(solution)/shard_map/ppermute | solution.py:26
  18.4 2.0 pad_maximum_fusion.6
  20.4 3.7 %fusion.50 = f32[8,128,512]{2,1,0:T(8,128)S(1)} fusion(bf16[8,512,128]{2,1,0:T(8,128)(2,1)S(1)} %bitcast.132, bf16[8,512,512]{2,1,0:T(8,128)(2,1)} %param.7), kind=kOutput, calls=%fused_computation.61 | convolution fusion | flops 536870912 | bytes 7340032 | tf_op jit(solution)/shard_map/bij,bjk->bik/dot_general | solution.py:44
  24.1 7.6 %fusion.41 = bf16[8,512,128]{1,2,0:T(8,128)(2,1)} fusion(bf16[1,8,512,512]{3,2,1,0:T(8,128)(2,1)} %param.6, bf16[8,512,128]{1,2,0:T(8,128)(2,1)S(1)} %copy.15, f32[8,128,512]{2,1,0:T(8,128)S(1)} %fusion.50, bf16[8,512,128]{2,1,0:T(8,128)(2,1)} %bitcast.139, bf16[8,512,512]{2,1,0:T(8,128)(2,1)} %param.8), kind=kOutput, calls=%fused_computation.30 | convolution fusion | flops 1076363264 | bytes 13631488 | tf_op jit(solution)/shard_map/bij,bjk->bik/dot_general | solution.py:50
  32.7 5.4 %collective-permute-start.2 = (bf16[512,128]{0,1:T(8,128)(2,1)S(1)}, bf16[512,128]{0,1:T(8,128)(2,1)S(1)}, u32[]{:S(2)}, u32[]{:S(2)}) collective-permute-start(bf16[512,128]{0,1:T(8,128)(2,1)S(1)} %get-tuple-element.16), channel_id=1, source_target_pairs={{0,1},{1,2},{2,3},{3,4},{4,5},{5,6},{6,7},{8,9},{9,10},{10,11},{11... | collective-permute-start | bytes 393224 | tf_op jit(solution)/shard_map/ppermute | solution.py:25
  39.4 1.6 copy.16
  42.6 3.7 %fusion.51 = f32[8,128,512]{2,1,0:T(8,128)S(1)} fusion(bf16[8,512,128]{2,1,0:T(8,128)(2,1)S(1)} %bitcast.133, bf16[8,512,512]{2,1,0:T(8,128)(2,1)} %param.7), kind=kOutput, calls=%fused_computation.62 | convolution fusion | flops 536870912 | bytes 7340032 | tf_op jit(solution)/shard_map/bij,bjk->bik/dot_general | solution.py:44
  46.3 7.6 %fusion.38 = bf16[8,512,128]{1,2,0:T(8,128)(2,1)} fusion(bf16[1,8,512,512]{3,2,1,0:T(8,128)(2,1)} %param.6, bf16[8,512,128]{1,2,0:T(8,128)(2,1)S(1)} %copy.15, f32[8,128,512]{2,1,0:T(8,128)S(1)} %fusion.51, bf16[8,512,128]{2,1,0:T(8,128)(2,1)} %bitcast.140, bf16[8,512,512]{2,1,0:T(8,128)(2,1)} %param.8), kind=kOutput, calls=%fused_computation.29 | convolution fusion | flops 1076363264 | bytes 13631488 | tf_op jit(solution)/shard_map/bij,bjk->bik/dot_general | solution.py:50
  55.0 5.0 %collective-permute-start.4 = (bf16[512,128]{0,1:T(8,128)(2,1)S(1)}, bf16[512,128]{0,1:T(8,128)(2,1)S(1)}, u32[]{:S(2)}, u32[]{:S(2)}) collective-permute-start(bf16[512,128]{0,1:T(8,128)(2,1)S(1)} %get-tuple-element.12), channel_id=1, source_target_pairs={{0,1},{1,2},{2,3},{3,4},{4,5},{5,6},{6,7},{8,9},{9,10},{10,11},{11... | collective-permute-start | bytes 393224 | tf_op jit(solution)/shard_map/ppermute | solution.py:25
  61.2 1.6 copy.19
  64.4 3.7 %fusion.52 = f32[8,128,512]{2,1,0:T(8,128)S(1)} fusion(bf16[8,512,128]{2,1,0:T(8,128)(2,1)S(1)} %bitcast.134, bf16[8,512,512]{2,1,0:T(8,128)(2,1)} %param.7), kind=kOutput, calls=%fused_computation.63 | convolution fusion | flops 536870912 | bytes 7340032 | tf_op jit(solution)/shard_map/bij,bjk->bik/dot_general | solution.py:44
  68.1 7.6 %fusion.35 = bf16[8,512,128]{1,2,0:T(8,128)(2,1)} fusion(bf16[1,8,512,512]{3,2,1,0:T(8,128)(2,1)} %param.6, bf16[8,512,128]{1,2,0:T(8,128)(2,1)S(1)} %copy.15, f32[8,128,512]{2,1,0:T(8,128)S(1)} %fusion.52, bf16[8,512,128]{2,1,0:T(8,128)(2,1)} %bitcast.141, bf16[8,512,512]{2,1,0:T(8,128)(2,1)} %param.8), kind=kOutput, calls=%fused_computation.28 | convolution fusion | flops 1076363264 | bytes 13631488 | tf_op jit(solution)/shard_map/bij,bjk->bik/dot_general | solution.py:50
  76.7 5.0 %collective-permute-start.6 = (bf16[512,128]{0,1:T(8,128)(2,1)S(1)}, bf16[512,128]{0,1:T(8,128)(2,1)S(1)}, u32[]{:S(2)}, u32[]{:S(2)}) collective-permute-start(bf16[512,128]{0,1:T(8,128)(2,1)S(1)} %get-tuple-element.8), channel_id=1, source_target_pairs={{0,1},{1,2},{2,3},{3,4},{4,5},{5,6},{6,7},{8,9},{9,10},{10,11},{11... | collective-permute-start | bytes 393224 | tf_op jit(solution)/shard_map/ppermute | solution.py:25
  86.8 3.7 %fusion.53 = f32[8,128,512]{2,1,0:T(8,128)S(1)} fusion(bf16[8,512,128]{2,1,0:T(8,128)(2,1)S(1)} %bitcast.135, bf16[8,512,512]{2,1,0:T(8,128)(2,1)} %param.7), kind=kOutput, calls=%fused_computation.64 | convolution fusion | flops 536870912 | bytes 7340032 | tf_op jit(solution)/shard_map/bij,bjk->bik/dot_general | solution.py:44
  90.5 8.0 %multiply_bitcast_fusion = f32[8,512,128]{1,2,0:T(8,128)} fusion(bf16[1,8,512,512]{3,2,1,0:T(8,128)(2,1)} %param.6, bf16[8,512,128]{1,2,0:T(8,128)(2,1)S(1)} %copy.15, f32[8,128,512]{2,1,0:T(8,128)S(1)} %fusion.53, bf16[8,512,128]{2,1,0:T(8,128)(2,1)} %bitcast.131, bf16[8,512,512]{2,1,0:T(8,128)(2,1)} %param.8, f32[]{:T(128)} %bitcast.129), kind=kOutput, calls=%fused_computation.22 | convolution fusion | flops 1077411840 | bytes 14680068 | tf_op jit(solution)/shard_map/bij,bjk->bik/dot_general | solution.py:50
  98.5 1.9 copy.25
  102.0 45.6 %collective-permute-done.8 = f32[4096,128]{1,0:T(8,128)S(1)} collective-permute-done((f32[4096,128]{1,0:T(8,128)S(1)}, f32[4096,128]{1,0:T(8,128)S(1)}, u32[]{:S(2)}, u32[]{:S(2)}) %collective-permute-start.8) | collective-permute-done | bytes 2097184 | tf_op jit(solution)/shard_map/ppermute | solution.py:13
  149.4 46.7 %collective-permute-done.9 = f32[4096,128]{1,0:T(8,128)S(1)} collective-permute-done((f32[4096,128]{1,0:T(8,128)S(1)}, f32[4096,128]{1,0:T(8,128)S(1)}, u32[]{:S(2)}, u32[]{:S(2)}) %collective-permute-start.9) | collective-permute-done | bytes 2097184 | tf_op jit(solution)/shard_map/ppermute | solution.py:13
  196.4 4.1 %fusion.54 = f32[128,128]{0,1:T(8,128)} fusion(f32[4096,128]{1,0:T(8,128)S(1)} %add.56), kind=kOutput, calls=%fused_computation.65 | convolution fusion | flops 805306368 | bytes 2162688 | tf_op jit(solution)/shard_map/dot_general | solution.py:58
  200.5 56.3 %all-reduce.2.cloned.1.call-done = f32[128,128]{0,1:T(8,128)} async-done(((f32[128,128]{0,1:T(8,128)}), f32[128,128]{0,1:T(8,128)}) %all-reduce.2.cloned.1.call-update) | async-done | bytes 65552 | tf_op jit(solution)/shard_map/psum | solution.py:59
  258.6 11.7 %cholesky.16 = f32[128,128]{1,0:T(8,128)S(1)} custom-call(f32[128,128]{1,0:T(8,128)S(1)} %fusion.48), custom_call_target="Cholesky" | custom-call | tf_op jit(solution)/shard_map/jit(cholesky)/cholesky | solution.py:61
  271.6 9.8 %custom-call.7 = f32[1,128,128]{1,2,0:T(8,128)S(1)} custom-call(f32[1,128,128]{2,1,0:T(8,128)S(1)} %fusion.46), custom_call_target="InvertDiagBlocksLowerTriangular" | custom-call | tf_op jit(solution)/shard_map/jit(_solve_triangular)/triangular_solve | solution.py:62
  (41 shorter events, 23.0 us)
Async XLA Ops:
  6.5 250.2 %all-reduce.2.cloned.1.call-start = ((), (), s32[]{:S(2)}) async-start(), calls=%async_computation | async-start | bytes 131072 | tf_op jit(solution)/shard_map/psum | solution.py:59
  6.5 7.6 %copy-start = (bf16[4096,128]{1,0:T(8,128)(2,1)S(1)}, bf16[4096,128]{1,0:T(8,128)(2,1)}, u32[]{:S(2)}) copy-start(bf16[4096,128]{1,0:T(8,128)(2,1)} %param.5) | copy-start | bytes 3145732
  10.4 4.3 %collective-permute-start = (bf16[512,128]{1,0:T(8,128)(2,1)S(1)}, bf16[512,128]{1,0:T(8,128)(2,1)S(1)}, u32[]{:S(2)}, u32[]{:S(2)}) collective-permute-start(bf16[512,128]{1,0:T(8,128)(2,1)S(1)} %get-tuple-element.20), channel_id=1, source_target_pairs={{0,1},{1,2},{2,3},{3,4},{4,5},{5,6},{6,7},{8,9},{9,10},{10,11},{11... | collective-permute-start | bytes 393224 | tf_op jit(solution)/shard_map/ppermute | solution.py:25
  12.8 5.5 %collective-permute-start.1 = (bf16[512,128]{1,0:T(8,128)(2,1)S(1)}, bf16[512,128]{1,0:T(8,128)(2,1)}, u32[]{:S(2)}, u32[]{:S(2)}) collective-permute-start(bf16[512,128]{1,0:T(8,128)(2,1)S(1)} %get-tuple-element.19), channel_id=1, source_target_pairs={{1,0},{2,1},{3,2},{4,3},{5,4},{6,5},{7,6},{9,8},{10,9},{11,10},{12... | collective-permute-start | bytes 393224 | tf_op jit(solution)/shard_map/ppermute | solution.py:26
  32.7 8.4 %collective-permute-start.2 = (bf16[512,128]{0,1:T(8,128)(2,1)S(1)}, bf16[512,128]{0,1:T(8,128)(2,1)S(1)}, u32[]{:S(2)}, u32[]{:S(2)}) collective-permute-start(bf16[512,128]{0,1:T(8,128)(2,1)S(1)} %get-tuple-element.16), channel_id=1, source_target_pairs={{0,1},{1,2},{2,3},{3,4},{4,5},{5,6},{6,7},{8,9},{9,10},{10,11},{11... | collective-permute-start | bytes 393224 | tf_op jit(solution)/shard_map/ppermute | solution.py:25
  38.1 3.2 %collective-permute-start.3 = (bf16[512,128]{0,1:T(8,128)(2,1)S(1)}, bf16[512,128]{0,1:T(8,128)(2,1)S(1)}, u32[]{:S(2)}, u32[]{:S(2)}) collective-permute-start(bf16[512,128]{0,1:T(8,128)(2,1)S(1)} %get-tuple-element.15), channel_id=1, source_target_pairs={{1,0},{2,1},{3,2},{4,3},{5,4},{6,5},{7,6},{9,8},{10,9},{11,10},{12... | collective-permute-start | bytes 393224 | tf_op jit(solution)/shard_map/ppermute | solution.py:26
  55.0 7.9 %collective-permute-start.4 = (bf16[512,128]{0,1:T(8,128)(2,1)S(1)}, bf16[512,128]{0,1:T(8,128)(2,1)S(1)}, u32[]{:S(2)}, u32[]{:S(2)}) collective-permute-start(bf16[512,128]{0,1:T(8,128)(2,1)S(1)} %get-tuple-element.12), channel_id=1, source_target_pairs={{0,1},{1,2},{2,3},{3,4},{4,5},{5,6},{6,7},{8,9},{9,10},{10,11},{11... | collective-permute-start | bytes 393224 | tf_op jit(solution)/shard_map/ppermute | solution.py:25
  59.9 3.2 %collective-permute-start.5 = (bf16[512,128]{0,1:T(8,128)(2,1)S(1)}, bf16[512,128]{0,1:T(8,128)(2,1)S(1)}, u32[]{:S(2)}, u32[]{:S(2)}) collective-permute-start(bf16[512,128]{0,1:T(8,128)(2,1)S(1)} %get-tuple-element.11), channel_id=1, source_target_pairs={{1,0},{2,1},{3,2},{4,3},{5,4},{6,5},{7,6},{9,8},{10,9},{11,10},{12... | collective-permute-start | bytes 393224 | tf_op jit(solution)/shard_map/ppermute | solution.py:26
  76.7 8.7 %collective-permute-start.6 = (bf16[512,128]{0,1:T(8,128)(2,1)S(1)}, bf16[512,128]{0,1:T(8,128)(2,1)S(1)}, u32[]{:S(2)}, u32[]{:S(2)}) collective-permute-start(bf16[512,128]{0,1:T(8,128)(2,1)S(1)} %get-tuple-element.8), channel_id=1, source_target_pairs={{0,1},{1,2},{2,3},{3,4},{4,5},{5,6},{6,7},{8,9},{9,10},{10,11},{11... | collective-permute-start | bytes 393224 | tf_op jit(solution)/shard_map/ppermute | solution.py:25
  81.7 3.9 %collective-permute-start.7 = (bf16[512,128]{0,1:T(8,128)(2,1)S(1)}, bf16[512,128]{0,1:T(8,128)(2,1)S(1)}, u32[]{:S(2)}, u32[]{:S(2)}) collective-permute-start(bf16[512,128]{0,1:T(8,128)(2,1)S(1)} %get-tuple-element.7), channel_id=1, source_target_pairs={{1,0},{2,1},{3,2},{4,3},{5,4},{6,5},{7,6},{9,8},{10,9},{11,10},{12... | collective-permute-start | bytes 393224 | tf_op jit(solution)/shard_map/ppermute | solution.py:26
  100.4 47.1 %collective-permute-start.8 = (f32[4096,128]{1,0:T(8,128)S(1)}, f32[4096,128]{1,0:T(8,128)S(1)}, u32[]{:S(2)}, u32[]{:S(2)}) collective-permute-start(f32[4096,128]{1,0:T(8,128)S(1)} %bitcast.130), channel_id=1, source_target_pairs={{0,8},{8,0},{16,24},{24,16},{1,9},{9,1},{17,25},{25,17},{2,10},{10... | collective-permute-start | bytes 6291464 | tf_op jit(solution)/shard_map/ppermute | solution.py:13
  147.8 48.3 %collective-permute-start.9 = (f32[4096,128]{1,0:T(8,128)S(1)}, f32[4096,128]{1,0:T(8,128)S(1)}, u32[]{:S(2)}, u32[]{:S(2)}) collective-permute-start(f32[4096,128]{1,0:T(8,128)S(1)} %bitcast_add_fusion.1), channel_id=1, source_target_pairs={{0,16},{8,24},{16,0},{24,8},{1,17},{9,25},{17,1},{25,9},{2,18},{10... | collective-permute-start | bytes 6291464 | tf_op jit(solution)/shard_map/ppermute | solution.py:13
Sparse Core Ops, SparseCore 0:
  200.6 56.1 all-reduce.1
